TPU v7x, 256 devices: a whole 4x4x8 slice. The times are simulated.
256 devices in a mesh: ia: 32 (over z, x_lo, core), ja: 4 (over y), ka: 2 (over x_hi).
Axes of the slice: x: 4 (x_hi: 2, x_lo: 2; x = x_hi * 2 + x_lo), y: 4, z: 8, core: 2. Of those that a mesh axis runs over, the one named last changes fastest.
Arguments:
- tensor: float32 [8192, 8, 8192], P('ja', 'ka', 'ia'), may hold values from -6 to 6
- factor_a: float32 [8192, 128], P('ia'), may hold values from -1 to 1
- factor_c: float32 [8, 128], P('ka'), may hold values from -2 to 2
- gram_c: float32 [128, 128], replicated, may hold values from -12 to 24, as said below
Outputs:
- factor_b: float32 [8192, 128], P('ja')
- factor_c_new: float32 [8, 128], P('ka')
Inputs may be any that keep to these rules, and one draw needn't show every extreme that they name: `gram_c`: symmetric positive definite.
All inputs are finite; a program needn't handle non-finite values.
Results may differ from a plain program's by a relative error of at most 0.000071.
Values sent between devices are 32-bit elements; how exact they have to be, the bound alone decides.
No kernel may reach another device: no remote copies, remote signals or barrier semaphores. Data moves between devices by JAX's collectives and lax.ppermute only.
A program may use at most 64 MiB of HBM per device.

v0:
```python
import jax
import jax.numpy as jnp
from jax import lax
from jax.sharding import PartitionSpec as P


def right_solve(rhs, system):
    lower = jnp.linalg.cholesky(system)
    middle = lax.linalg.triangular_solve(lower, rhs, left_side=False, lower=True, transpose_a=True)
    return lax.linalg.triangular_solve(
        lower, middle, left_side=False, lower=True, transpose_a=False
    )


def body(tensor, factor_a, factor_c, gram_c):
    high = lax.Precision.HIGHEST
    mode_two, mode_three, mode_one = tensor.shape
    rank = factor_a.shape[1]
    gram_a = lax.psum(
        jnp.dot(factor_a.T, factor_a, precision=high, preferred_element_type=jnp.float32), "ia"
    )
    system_b = gram_a * gram_c
    count = mode_two // lax.axis_size("ia") * lax.axis_size("ia")
    flat = jnp.dot(
        tensor.reshape(count * mode_three, mode_one),
        factor_a,
        precision=high,
        preferred_element_type=jnp.float32,
    )
    shares = lax.psum_scatter(
        flat.reshape(count, mode_three, rank), "ia", scatter_dimension=0, tiled=True
    )
    local_b = lax.psum(jnp.sum(shares * factor_c[None, :, :], axis=1), "ka")
    rows_b = right_solve(local_b, system_b)
    local_c = jnp.sum(shares * rows_b[:, None, :], axis=0)
    local_gram = jnp.dot(rows_b.T, rows_b, precision=high, preferred_element_type=jnp.float32)
    mttkrp_c, gram_b = lax.psum((local_c, local_gram), ("ia", "ja"))
    factor_b = lax.all_gather(rows_b, "ia", axis=0, tiled=True)
    factor_c_new = right_solve(mttkrp_c, gram_a * gram_b)
    return (factor_b, factor_c_new)


def solution(mesh):
    placed = (P("ja", "ka", "ia"), P("ia", None), P("ka", None), P())
    return jax.shard_map(
        body, mesh=mesh, in_specs=placed, out_specs=(P("ja", None), P("ka", None)), check_vma=False
    )
```

profile of v0, /device:TPU:1, one launch (start us, length us, event | category | flops | bytes accessed | tf_op | source)
XLA Modules:
  0.0 1342.1 jit_solution(12914689093623090301)
XLA Ops:
  7.2 0.8 copy-done
  8.1 1.0 fusion.15
  9.2 11.6 fusion
  20.9 186.3 %all-reduce.3.cloned.1.call-done = f32[128,128]{0,1:T(8,128)} async-done(((f32[128,128]{0,1:T(8,128)}), f32[128,128]{0,1:T(8,128)}) %all-reduce.3.cloned.1.call-update) | async-done | bytes 65552 | tf_op jit(solution)/shard_map/psum | solution.py:19
  207.2 0.8 mul.24
  208.2 11.7 cholesky.44
  220.0 0.6 compare_reduce_fusion.1
  220.6 0.7 fusion.3
  221.3 9.8 custom-call.12
  231.1 97.8 %reduce-scatter.2.cloned.1.call-done = f32[64,4,128]{2,0,1:T(8,128)} async-done(((f32[2048,4,128]{2,0,1:T(8,128)}), f32[64,4,128]{2,0,1:T(8,128)}) %reduce-scatter.2.cloned.1.call-update) | async-done | bytes 131088 | tf_op jit(solution)/shard_map/reduce_scatter | solution.py:30
  328.9 0.9 multiply_reduce_fusion.1
  329.9 9.2 psum.28
  339.5 0.9 fusion.16
  341.0 0.9 multiply_reduce_fusion
  341.9 277.2 %psum.30 = f32[4,128]{1,0:T(4,128)S(1)} all-reduce(f32[4,128]{1,0:T(4,128)S(1)} %multiply_reduce_fusion), channel_id=1, replica_groups=mesh['ia'=32,'ja'=4,'ka'=2] {'ia','ja'}, use_global_device_ids=true, to_apply=%region_7.9 | all-reduce | flops 512 | bytes 4096 | tf_op jit(solution)/shard_map/psum | solution.py:37
  619.1 650.4 %all-reduce.5.cloned.1.call-done = f32[128,128]{0,1:T(8,128)} async-done(((f32[128,128]{0,1:T(8,128)}), f32[128,128]{0,1:T(8,128)}) %all-reduce.5.cloned.1.call-update) | async-done | bytes 65552 | tf_op jit(solution)/shard_map/psum | solution.py:37
  1269.6 0.9 mul.27
  1270.6 11.7 cholesky.55
  1282.3 0.6 compare_reduce_fusion
  1282.9 0.7 fusion.4
  1283.6 9.8 custom-call.13
  1293.6 0.8 fusion.5
  1294.4 38.9 %all-gather.2.cloned.1.call-done = f32[2048,128]{1,0:T(8,128)} async-done(((f32[64,128]{1,0:T(8,128)}), f32[2048,128]{1,0:T(8,128)}) %all-gather.2.cloned.1.call-update) | async-done | bytes 1048592 | tf_op jit(solution)/shard_map/all_gather | solution.py:38
  1333.3 2.3 copy.19
  (25 shorter events, 1.7 us)
Async XLA Ops:
  7.2 0.9 copy-start
  7.2 200.1 %all-reduce.3.cloned.1.call-start = ((), (), s32[]{:S(2)}) async-start(), calls=%async_computation.2 | async-start | bytes 131072 | tf_op jit(solution)/shard_map/psum | solution.py:19
  9.1 11.7 copy-start.2
  9.1 319.8 %copy-start.3 = (f32[4,128]{1,0:T(4,128)S(1)}, f32[4,128]{1,0:T(4,128)}, u32[]{:S(2)}) copy-start(f32[4,128]{1,0:T(4,128)} %param.7) | copy-start | bytes 6148
  9.1 319.8 %reduce-scatter.2.cloned.1.call-start = ((), (), s32[]{:S(2)}) async-start(), calls=%async_computation.1 | async-start | bytes 4325376 | tf_op jit(solution)/shard_map/reduce_scatter | solution.py:30
  20.8 1248.8 %all-reduce.5.cloned.1.call-start = ((), (), s32[]{:S(2)}) async-start(), calls=%async_computation.4 | async-start | bytes 131072 | tf_op jit(solution)/shard_map/psum | solution.py:37
  339.5 1.0 copy-start.1
  340.4 992.9 %all-gather.2.cloned.1.call-start = ((), (), s32[]{:S(2)}) async-start(), calls=%async_computation.3 | async-start | bytes 1081344 | tf_op jit(solution)/shard_map/all_gather | solution.py:38
Sparse Core Ops, SparseCore 0:
  11.2 195.9 all-reduce.2
  209.9 118.9 reduce-scatter.1
  340.5 928.9 all-reduce.4
  1271.3 61.9 all-gather.1
where the time goes:
time: 1340 us
  waiting for transfers between devices  974 us (73%)
  blocking collectives  286 us (21%)
  other arithmetic  49.3 us (4%)
  matrix products  14.9 us (1%)
  between operations  13.9 us (1%)
    psum x1, waiting for transfers between devices, body(): mttkrp_c, gram_b = lax.psum((local_c, local_gram), ('ia', 'ja'))  650 us
    psum x1, blocking collectives, body(): mttkrp_c, gram_b = lax.psum((local_c, local_gram), ('ia', 'ja'))  277 us
    psum x1, waiting for transfers between devices, body(): lax.psum(jnp.dot(factor_a.T, factor_a, precision=high, preferred_element_...  186 us
    reduce_scatter x1, waiting for transfers between devices, body(): lax.psum_scatter(flat.reshape(count, mode_three, rank), 'ia', scatter_dim...  97.8 us
    all_gather x1, waiting for transfers between devices, body(): factor_b = lax.all_gather(rows_b, 'ia', axis=0, tiled=True)  38.9 us
  transfers between devices with their start and end apart: 4, of which 4 were waited for; matrix products, arithmetic and copies ran while one was open for 5% of the time, Pallas kernels for 0%

commit v1 on v0

--- a/solution.py
+++ b/solution.py
@@ -34,7 +34,7 @@
     rows_b = right_solve(local_b, system_b)
     local_c = jnp.sum(shares * rows_b[:, None, :], axis=0)
     local_gram = jnp.dot(rows_b.T, rows_b, precision=high, preferred_element_type=jnp.float32)
-    mttkrp_c, gram_b = lax.psum((local_c, local_gram), ("ia", "ja"))
+    mttkrp_c, gram_b = lax.psum(lax.psum((local_c, local_gram), "ia"), "ja")
     factor_b = lax.all_gather(rows_b, "ia", axis=0, tiled=True)
     factor_c_new = right_solve(mttkrp_c, gram_a * gram_b)
     return (factor_b, factor_c_new)

time: 1340 us -> 658 us (0.49)
  waiting for transfers between devices: 974 us -> 504 us
  blocking collectives: 286 us -> 71.7 us
    psum x1 -> x2, waiting for transfers between devices: 650 us -> 194 us  [body(): mttkrp_c, gram_b = lax.psum(lax.psum((local_c, local_gram), 'ia'), 'ja')]
    psum x1 -> x2, blocking collectives: 277 us -> 62.5 us  [body(): mttkrp_c, gram_b = lax.psum(lax.psum((local_c, local_gram), 'ia'), 'ja')]
    all_gather x1, waiting for transfers between devices: 38.9 us -> 25.3 us  [body(): factor_b = lax.all_gather(rows_b, 'ia', axis=0, tiled=True)]
  transfers between devices with their start and end apart: 4 -> 5, of which waited for: 4 -> 4; matrix products, arithmetic and copies ran while one was open for 5% -> 9% of each run, Pallas kernels for 0% -> 0%
where the time goes in v1:
time: 658 us
  waiting for transfers between devices  504 us (77%)
  blocking collectives  71.7 us (11%)
  other arithmetic  49.3 us (7%)
  matrix products  14.9 us (2%)
  between operations  13.9 us (2%)
    psum x2, waiting for transfers between devices, body(): mttkrp_c, gram_b = lax.psum(lax.psum((local_c, local_gram), 'ia'), 'ja')  194 us
    psum x1, waiting for transfers between devices, body(): lax.psum(jnp.dot(factor_a.T, factor_a, precision=high, preferred_element_...  186 us
    reduce_scatter x1, waiting for transfers between devices, body(): lax.psum_scatter(flat.reshape(count, mode_three, rank), 'ia', scatter_dim...  97.8 us
    psum x2, blocking collectives, body(): mttkrp_c, gram_b = lax.psum(lax.psum((local_c, local_gram), 'ia'), 'ja')  62.5 us
    all_gather x1, waiting for transfers between devices, body(): factor_b = lax.all_gather(rows_b, 'ia', axis=0, tiled=True)  25.3 us
    another operation x6, other arithmetic, right_solve(): lower = jnp.linalg.cholesky(system)  24.8 us
    another operation x4, other arithmetic, right_solve(): lax.linalg.triangular_solve(lower, rhs, left_side=False, lower=True, tran...  20.9 us
  transfers between devices with their start and end apart: 5, of which 4 were waited for; matrix products, arithmetic and copies ran while one was open for 9% of the time, Pallas kernels for 0%

profile of v1, /device:TPU:1, one launch (start us, length us, event | category | flops | bytes accessed | tf_op | source)
XLA Modules:
  0.0 657.5 jit_solution(6715284974032281165)
XLA Ops:
  7.2 0.8 copy-done
  8.1 1.0 fusion.15
  9.2 11.6 %fusion = f32[2048,4,128]{2,0,1:T(8,128)} fusion(f32[2048,4,256]{2,1,0:T(4,128)} %param.5, f32[256,128]{1,0:T(8,128)S(1)} %copy-done), kind=kOutput, calls=%fused_computation | convolution fusion | flops 3221225472 | bytes 12713984 | tf_op jit(solution)/shard_map/dot_general | solution.py:24
  20.9 186.3 %all-reduce.4.cloned.1.call-done = f32[128,128]{0,1:T(8,128)} async-done(((f32[128,128]{0,1:T(8,128)}), f32[128,128]{0,1:T(8,128)}) %all-reduce.4.cloned.1.call-update) | async-done | bytes 65552 | tf_op jit(solution)/shard_map/psum | solution.py:19
  207.2 0.8 mul.24
  208.2 11.7 %cholesky.44 = f32[128,128]{1,0:T(8,128)S(1)} custom-call(f32[128,128]{1,0:T(8,128)S(1)} %fusion.14), custom_call_target="Cholesky" | custom-call | tf_op jit(solution)/shard_map/jit(cholesky)/cholesky | solution.py:8
  220.0 0.6 compare_reduce_fusion.1
  220.6 0.7 fusion.3
  221.3 9.8 %custom-call.12 = f32[1,128,128]{1,2,0:T(8,128)S(1)} custom-call(f32[1,128,128]{2,1,0:T(8,128)S(1)} %fusion.3), custom_call_target="InvertDiagBlocksLowerTriangular" | custom-call | tf_op jit(solution)/shard_map/triangular_solve | solution.py:9
  231.1 97.8 %reduce-scatter.2.cloned.1.call-done = f32[64,4,128]{2,0,1:T(8,128)} async-done(((f32[2048,4,128]{2,0,1:T(8,128)}), f32[64,4,128]{2,0,1:T(8,128)}) %reduce-scatter.2.cloned.1.call-update) | async-done | bytes 131088 | tf_op jit(solution)/shard_map/reduce_scatter | solution.py:30
  328.9 0.9 multiply_reduce_fusion.1
  329.9 9.2 %psum.42 = f32[64,128]{1,0:T(8,128)S(1)} all-reduce(f32[64,128]{1,0:T(8,128)S(1)} %multiply_reduce_fusion.1), channel_id=1, replica_groups=mesh['ia'=32,'ja'=4,'ka'=2] {'ka'}, use_global_device_ids=true, to_apply=%region_2.0 | all-reduce | flops 8192 | bytes 65536 | tf_op jit(solution)/shard_map/psum | solution.py:33
  339.5 0.9 fusion.16
  340.5 194.0 %all-reduce.6.cloned.1.call-done = f32[128,128]{0,1:T(8,128)} async-done(((f32[128,128]{0,1:T(8,128)}), f32[128,128]{0,1:T(8,128)}) %all-reduce.6.cloned.1.call-update) | async-done | bytes 65552 | tf_op jit(solution)/shard_map/psum | solution.py:37
  535.1 0.9 multiply_reduce_fusion
  536.0 54.2 %psum.44 = f32[4,128]{1,0:T(4,128)S(1)} all-reduce(f32[4,128]{1,0:T(4,128)S(1)} %multiply_reduce_fusion), channel_id=1, replica_groups=mesh['ia'=32,'ja'=4,'ka'=2] {'ia'}, use_global_device_ids=true, to_apply=%region_7.0 | all-reduce | flops 512 | bytes 4096 | tf_op jit(solution)/shard_map/psum | solution.py:37
  590.2 8.3 %psum.45 = f32[4,128]{1,0:T(4,128)S(1)} all-reduce(f32[4,128]{1,0:T(4,128)S(1)} %psum.44), channel_id=1, replica_groups=mesh['ia'=32,'ja'=4,'ka'=2] {'ja'}, use_global_device_ids=true, to_apply=%region_8.0 | all-reduce | flops 512 | bytes 4096 | tf_op jit(solution)/shard_map/psum | solution.py:37
  598.6 0.9 mul.27
  599.6 11.7 %cholesky.55 = f32[128,128]{1,0:T(8,128)S(1)} custom-call(f32[128,128]{1,0:T(8,128)S(1)} %fusion.9), custom_call_target="Cholesky" | custom-call | tf_op jit(solution)/shard_map/jit(cholesky)/cholesky | solution.py:8
  612.0 0.7 fusion.4
  612.6 9.8 %custom-call.13 = f32[1,128,128]{1,2,0:T(8,128)S(1)} custom-call(f32[1,128,128]{2,1,0:T(8,128)S(1)} %fusion.4), custom_call_target="InvertDiagBlocksLowerTriangular" | custom-call | tf_op jit(solution)/shard_map/triangular_solve | solution.py:9
  622.6 0.8 fusion.5
  623.4 25.3 %all-gather.2.cloned.1.call-done = f32[2048,128]{1,0:T(8,128)} async-done(((f32[64,128]{1,0:T(8,128)}), f32[2048,128]{1,0:T(8,128)}) %all-gather.2.cloned.1.call-update) | async-done | bytes 1048592 | tf_op jit(solution)/shard_map/all_gather | solution.py:38
  648.7 2.3 copy.20
  (29 shorter events, 2.4 us)
Async XLA Ops:
  7.2 0.9 copy-start
  7.2 200.1 %all-reduce.4.cloned.1.call-start = ((), (), s32[]{:S(2)}) async-start(), calls=%async_computation.2 | async-start | bytes 131072 | tf_op jit(solution)/shard_map/psum | solution.py:19
  9.1 11.7 %copy-start.2 = (f32[128,128]{1,0:T(8,128)S(1)}, f32[128,128]{1,0:T(8,128)}, u32[]{:S(2)}) copy-start(f32[128,128]{1,0:T(8,128)} %param.8) | copy-start | bytes 196612
  9.1 319.8 %copy-start.3 = (f32[4,128]{1,0:T(4,128)S(1)}, f32[4,128]{1,0:T(4,128)}, u32[]{:S(2)}) copy-start(f32[4,128]{1,0:T(4,128)} %param.7) | copy-start | bytes 6148
  9.1 319.8 %reduce-scatter.2.cloned.1.call-start = ((), (), s32[]{:S(2)}) async-start(), calls=%async_computation.1 | async-start | bytes 4325376 | tf_op jit(solution)/shard_map/reduce_scatter | solution.py:30
  20.8 513.7 %all-reduce.6.cloned.1.call-start = ((), (), s32[]{:S(2)}) async-start(), calls=%async_computation.4 | async-start | bytes 131072 | tf_op jit(solution)/shard_map/psum | solution.py:37
  339.5 195.1 %copy-start.1 = (f32[64,128]{1,0:T(8,128)}, f32[64,128]{1,0:T(8,128)S(1)}, u32[]{:S(2)}) copy-start(f32[64,128]{1,0:T(8,128)S(1)} %fusion.10) | copy-start | bytes 98308
  340.4 258.1 %all-reduce.8.cloned.1.call-start = ((), (), s32[]{:S(2)}) async-start(), calls=%async_computation.5 | async-start | bytes 131072 | tf_op jit(solution)/shard_map/psum | solution.py:37
  534.5 114.2 %all-gather.2.cloned.1.call-start = ((), (), s32[]{:S(2)}) async-start(), calls=%async_computation.3 | async-start | bytes 1081344 | tf_op jit(solution)/shard_map/all_gather | solution.py:38
Sparse Core Ops, SparseCore 0:
  11.2 195.9 all-reduce.3
  209.9 118.9 reduce-scatter.1
  340.5 193.8 all-reduce.5
  536.6 43.4 all-reduce.7
  582.0 66.6 all-gather.1
